TPU v7x, 256 devices: a whole 4x4x8 slice. The times are simulated.
256 devices in a mesh: tm: 8 (over x_lo, y), sta: 32 (over x_hi, z, core).
Axes of the slice: x: 4 (x_hi: 2, x_lo: 2; x = x_hi * 2 + x_lo), y: 4, z: 8, core: 2. Of those that a mesh axis runs over, the one named last changes fastest.
Arguments:
- templates: bfloat16 [8, 256, 32, 3, 600], P('tm', None, 'sta'), may hold values from -6 to 6
- channel_mask: int32 [8, 256, 32], P('tm', None, 'sta'), may hold values 0 or 1
- waveforms: bfloat16 [32, 3, 7168], P('sta', None, 'tm'), may hold values from -60 to 60
- waveform_tail: bfloat16 [32, 3, 599], P('sta'), may hold values from -6 to 6
Outputs:
- detections: float32 [8, 256, 7168], P(None, 'sta', 'tm')
All inputs are finite; a program needn't handle non-finite values. No bound on the sum of `channel_mask` on one device may be relied on, other than what follows from the above.
Results may differ from a plain program's by a relative error of at most 0.0044.
Values may be sent and summed in bfloat16 or wider, within the bound.
A program may use at most 128 MiB of HBM per device.

v0:
```python
import jax
import jax.numpy as jnp
from jax import lax
from jax.sharding import PartitionSpec as P


def from_behind(x, axis, by):
    size = lax.axis_size(axis)
    pairs = [(i, i + by) for i in range(size) if 0 <= i + by < size]
    return lax.ppermute(x, axis, pairs)


def from_behind_2(x, axis, by):
    size = lax.axis_size(axis)
    return lax.ppermute(x, axis, [(i, (i + by) % size) for i in range(size)])


def normalize(templates, channel_mask):
    values = templates.astype(jnp.float32)
    centred = values - jnp.mean(values, axis=-1, keepdims=True)
    energy = jnp.sum(centred * centred, axis=-1, keepdims=True)
    weighted = (
        centred * lax.rsqrt(energy + 1e-05) * channel_mask.astype(jnp.float32)[..., None, None]
    )
    return weighted.astype(jnp.bfloat16)


def windows(extended, length, sample_count):
    values = extended.astype(jnp.float32)
    zero_col = jnp.zeros(values.shape[:-1] + (1,), jnp.float32)
    prefix_one = jnp.concatenate([zero_col, jnp.cumsum(values, axis=-1)], axis=-1)
    prefix_two = jnp.concatenate([zero_col, jnp.cumsum(values * values, axis=-1)], axis=-1)
    window_sum = prefix_one[..., length : length + sample_count] - prefix_one[..., :sample_count]
    window_square = prefix_two[..., length : length + sample_count] - prefix_two[..., :sample_count]
    inverse = lax.rsqrt(window_square - window_sum * window_sum / length + 1e-05)
    span = extended.shape[-1]
    leading = extended.shape[:-1]
    copies = jnp.broadcast_to(extended[..., None, :], leading + (length + 1, span))
    flat = copies.reshape(leading + ((length + 1) * span,))
    hankel = flat[..., : length * (span + 1)].reshape(leading + (length, span + 1))[
        ..., :sample_count
    ]
    return (hankel.astype(jnp.float32) * inverse[..., None, :]).astype(jnp.bfloat16)


def stacked(tpl_block, scaled):
    return lax.psum_scatter(
        jnp.dot(tpl_block, scaled, preferred_element_type=jnp.float32),
        "sta",
        scatter_dimension=0,
        tiled=True,
    )


def per_device(templates, channel_mask, waveforms, waveform_tail):
    length = templates.shape[-1]
    sample_count = waveforms.shape[-1]
    tm_count = lax.axis_size("tm")
    sta_count = lax.axis_size("sta")
    tm_index = lax.axis_index("tm")
    normed = normalize(templates, channel_mask)[0]
    tpl_rows = normed.shape[0]
    tpl_flat = normed.reshape(tpl_rows, -1)
    own_rows = tpl_rows // sta_count
    following = from_behind(waveforms[:, :, : length - 1], "tm", -1)
    following = jnp.where(tm_index == tm_count - 1, waveform_tail, following)
    extended = jnp.concatenate([waveforms, following], axis=-1)
    scaled = windows(extended, length, sample_count).reshape(-1, sample_count)
    result = jnp.zeros((tm_count, own_rows, sample_count), jnp.float32)
    tpl_block = tpl_flat
    for turn_index in range(tm_count):
        if turn_index > 0:
            tpl_block = from_behind_2(tpl_block, "tm", 1)
        anchor = (tm_index - turn_index) % tm_count
        result = lax.dynamic_update_index_in_dim(result, stacked(tpl_block, scaled), anchor, 0)
    return result


def solution(mesh):
    placed = (
        P("tm", None, "sta", None, None),
        P("tm", None, "sta"),
        P("sta", None, "tm"),
        P("sta", None, None),
    )
    return jax.shard_map(
        per_device, mesh=mesh, in_specs=placed, out_specs=P(None, "sta", "tm"), check_vma=False
    )
```

profile of v0, /device:TPU:26, one launch (start us, length us, event | category | flops | bytes accessed | tf_op | source)
XLA Modules:
  0.0 515.8 jit_solution(7613664675636639910)
XLA Ops:
  6.5 1.4 convert_reduce_fusion
  7.9 1.4 fusion.2
  10.0 1.5 fusion.4
  11.5 2.0 collective-permute-start.1
  13.5 20.2 %collective-permute-done.1 = bf16[256,1800]{0,1:T(8,128)(2,1)S(1)} collective-permute-done((bf16[256,1800]{0,1:T(8,128)(2,1)S(1)}, bf16[256,1800]{0,1:T(8,128)(2,1)S(1)}, u32[]{:S(2)}, u32[]{:S(2)}) %collective-permute-start.1) | collective-permute-done | bytes 921632 | tf_op jit(solution)/shard_map/ppermute | solution.py:15
  33.8 2.4 collective-permute-start.2
  36.2 18.9 %collective-permute-done.2 = bf16[256,1800]{0,1:T(8,128)(2,1)S(1)} collective-permute-done((bf16[256,1800]{0,1:T(8,128)(2,1)S(1)}, bf16[256,1800]{0,1:T(8,128)(2,1)S(1)}, u32[]{:S(2)}, u32[]{:S(2)}) %collective-permute-start.2) | collective-permute-done | bytes 921632 | tf_op jit(solution)/shard_map/ppermute | solution.py:15
  55.1 2.8 collective-permute-start.3
  57.9 17.7 %collective-permute-done.3 = bf16[256,1800]{0,1:T(8,128)(2,1)} collective-permute-done((bf16[256,1800]{0,1:T(8,128)(2,1)S(1)}, bf16[256,1800]{0,1:T(8,128)(2,1)}, u32[]{:S(2)}, u32[]{:S(2)}) %collective-permute-start.3) | collective-permute-done | bytes 921632 | tf_op jit(solution)/shard_map/ppermute | solution.py:15
  75.6 3.2 collective-permute-start.4
  85.1 10.3 %collective-permute-done.4 = bf16[256,1800]{0,1:T(8,128)(2,1)} collective-permute-done((bf16[256,1800]{0,1:T(8,128)(2,1)}, bf16[256,1800]{0,1:T(8,128)(2,1)}, u32[]{:S(2)}, u32[]{:S(2)}) %collective-permute-start.4) | collective-permute-done | bytes 921632 | tf_op jit(solution)/shard_map/ppermute | solution.py:15
  95.3 4.1 collective-permute-start.5
  99.6 2.8 broadcast_in_dim.44
  102.4 16.4 %reshape.181 = bf16[2695485]{0:T(1024)(128)(2,1)} reshape(bf16[3,601,1495]{2,1,0:T(8,128)(2,1)} %broadcast_in_dim.44) | data formatting | bytes 10781940
  118.8 8.9 %broadcast_in_dim.45 = bf16[1,3,898495]{2,1,0:T(4,128)(2,1)} reshape(bf16[2695485]{0:T(1024)(128)(2,1)} %reshape.181) | data formatting | bytes 10781940 | tf_op jit(solution)/shard_map/broadcast_in_dim | solution.py:38
  127.7 7.3 %slice.54 = bf16[1,3,897600]{2,1,0:T(4,128)(2,1)} slice(bf16[1,3,898495]{2,1,0:T(4,128)(2,1)} %broadcast_in_dim.45), slice={[0:1], [0:3], [0:897600]} | slice | bytes 10771200 | tf_op jit(solution)/shard_map/slice | solution.py:40
  135.0 12.3 %reshape.183 = bf16[2692800]{0:T(1024)(128)(2,1)} reshape(bf16[1,3,897600]{2,1,0:T(4,128)(2,1)} %slice.54) | data formatting | bytes 10771200
  147.3 11.9 %reshape.157 = bf16[1,3,600,1496]{3,2,1,0:T(8,128)(2,1)} reshape(bf16[2692800]{0:T(1024)(128)(2,1)} %reshape.183) | data formatting | bytes 10771200 | tf_op jit(solution)/shard_map/reshape | solution.py:40
  159.1 2.6 multiply_convert_fusion
  161.7 2.2 fusion.19
  164.1 2.2 fusion.20
  166.3 2.2 fusion.21
  168.6 3.4 fusion.22
  172.0 9.0 %collective-permute-done.6 = bf16[256,1800]{0,1:T(8,128)(2,1)S(1)} collective-permute-done((bf16[256,1800]{0,1:T(8,128)(2,1)}, bf16[256,1800]{0,1:T(8,128)(2,1)S(1)}, u32[]{:S(2)}, u32[]{:S(2)}) %collective-permute-start.6) | collective-permute-done | bytes 921632 | tf_op jit(solution)/shard_map/ppermute | solution.py:15
  181.0 3.9 collective-permute-start.7
  184.9 3.4 fusion.23
  188.3 3.4 fusion.24
  191.8 2.3 fusion.25
  194.1 6.6 %collective-permute-done.7 = bf16[256,1800]{0,1:T(8,128)(2,1)S(1)} collective-permute-done((bf16[256,1800]{0,1:T(8,128)(2,1)S(1)}, bf16[256,1800]{0,1:T(8,128)(2,1)S(1)}, u32[]{:S(2)}, u32[]{:S(2)}) %collective-permute-start.7) | collective-permute-done | bytes 921632 | tf_op jit(solution)/shard_map/ppermute | solution.py:15
  200.6 2.2 fusion.26
  204.8 296.6 %all-reduce.15.cloned.1.call-done = (f32[256,896]{1,0:T(8,128)}, f32[256,896]{1,0:T(8,128)}, f32[256,896]{1,0:T(8,128)}, f32[256,896]{1,0:T(8,128)}, f32[256,896...) async-done(((f32[256,896]{1,0:T(8,128)}, f32[256,896]{1,0:T(8,128)}, f32[256,896]{1,0:T(8,128)}, f32[256,896]{1,0:T(8,128)}, ...) | async-done | bytes 7340048
  507.4 1.4 fusion.5
  (54 shorter events, 14.3 us)
Async XLA Ops:
  6.5 72.2 %copy-start.1 = (bf16[1,3,896]{2,1,0:T(4,128)(2,1)S(1)}, bf16[1,3,896]{2,1,0:T(4,128)(2,1)}, u32[]{:S(2)}) copy-start(bf16[1,3,896]{2,1,0:T(4,128)(2,1)} %param.6) | copy-start | bytes 16132
  6.5 74.9 %copy-start.2 = (bf16[1,3,599]{2,1,0:T(4,128)(2,1)S(1)}, bf16[1,3,599]{2,1,0:T(4,128)(2,1)}, u32[]{:S(2)}) copy-start(bf16[1,3,599]{2,1,0:T(4,128)(2,1)} %param.7) | copy-start | bytes 10786
  6.5 494.9 %all-reduce.15.cloned.1.call-start = ((), (), s32[]{:S(2)}) async-start(), calls=%async_computation | async-start | bytes 14680064
  11.5 22.3 %collective-permute-start.1 = (bf16[256,1800]{0,1:T(8,128)(2,1)S(1)}, bf16[256,1800]{0,1:T(8,128)(2,1)S(1)}, u32[]{:S(2)}, u32[]{:S(2)}) collective-permute-start(bf16[256,1800]{0,1:T(8,128)(2,1)S(1)} %bitcast.77), channel_id=1, source_target_pairs={{0,32},{32,64},{64,96},{96,128},{128,160},{160,192},{192,224},{224... | collective-permute-start | bytes 2764808 | tf_op jit(solution)/shard_map/ppermute | solution.py:15
  33.8 21.3 %collective-permute-start.2 = (bf16[256,1800]{0,1:T(8,128)(2,1)S(1)}, bf16[256,1800]{0,1:T(8,128)(2,1)S(1)}, u32[]{:S(2)}, u32[]{:S(2)}) collective-permute-start(bf16[256,1800]{0,1:T(8,128)(2,1)S(1)} %collective-permute-done.1), channel_id=1, source_target_pairs={{0,32},{32,64},{64,96},{96,128},{128,160},{160,192},{192,224},{224... | collective-permute-start | bytes 2764808 | tf_op jit(solution)/shard_map/ppermute | solution.py:15
  55.1 20.5 %collective-permute-start.3 = (bf16[256,1800]{0,1:T(8,128)(2,1)S(1)}, bf16[256,1800]{0,1:T(8,128)(2,1)}, u32[]{:S(2)}, u32[]{:S(2)}) collective-permute-start(bf16[256,1800]{0,1:T(8,128)(2,1)S(1)} %collective-permute-done.2), channel_id=1, source_target_pairs={{0,32},{32,64},{64,96},{96,128},{128,160},{160,192},{192,224},{224... | collective-permute-start | bytes 2764808 | tf_op jit(solution)/shard_map/ppermute | solution.py:15
  75.6 19.8 %collective-permute-start.4 = (bf16[256,1800]{0,1:T(8,128)(2,1)}, bf16[256,1800]{0,1:T(8,128)(2,1)}, u32[]{:S(2)}, u32[]{:S(2)}) collective-permute-start(bf16[256,1800]{0,1:T(8,128)(2,1)} %collective-permute-done.3), channel_id=1, source_target_pairs={{0,32},{32,64},{64,96},{96,128},{128,160},{160,192},{192,224},{224... | collective-permute-start | bytes 2764808 | tf_op jit(solution)/shard_map/ppermute | solution.py:15
  78.8 2.6 collective-permute-start
  95.3 68.6 %collective-permute-start.5 = (bf16[256,1800]{0,1:T(8,128)(2,1)}, bf16[256,1800]{0,1:T(8,128)(2,1)}, u32[]{:S(2)}, u32[]{:S(2)}) collective-permute-start(bf16[256,1800]{0,1:T(8,128)(2,1)} %collective-permute-done.4), channel_id=1, source_target_pairs={{0,32},{32,64},{64,96},{96,128},{128,160},{160,192},{192,224},{224... | collective-permute-start | bytes 2764808 | tf_op jit(solution)/shard_map/ppermute | solution.py:15
  163.9 17.1 %collective-permute-start.6 = (bf16[256,1800]{0,1:T(8,128)(2,1)}, bf16[256,1800]{0,1:T(8,128)(2,1)S(1)}, u32[]{:S(2)}, u32[]{:S(2)}) collective-permute-start(bf16[256,1800]{0,1:T(8,128)(2,1)} %collective-permute-done.5), channel_id=1, source_target_pairs={{0,32},{32,64},{64,96},{96,128},{128,160},{160,192},{192,224},{224... | collective-permute-start | bytes 2764808 | tf_op jit(solution)/shard_map/ppermute | solution.py:15
  181.0 19.6 %collective-permute-start.7 = (bf16[256,1800]{0,1:T(8,128)(2,1)S(1)}, bf16[256,1800]{0,1:T(8,128)(2,1)S(1)}, u32[]{:S(2)}, u32[]{:S(2)}) collective-permute-start(bf16[256,1800]{0,1:T(8,128)(2,1)S(1)} %collective-permute-done.6), channel_id=1, source_target_pairs={{0,32},{32,64},{64,96},{96,128},{128,160},{160,192},{192,224},{224... | collective-permute-start | bytes 2764808 | tf_op jit(solution)/shard_map/ppermute | solution.py:15
  202.9 0.7 copy-start.3
  506.7 0.7 copy-start
Sparse Core Ops, SparseCore 0:
  203.0 298.3 all-reduce.14
where the time goes:
time: 523 us; the launch traced here: 516 us
  waiting for transfers between devices  381 us (73%)
  local copies, waits for them, and re-layouts  68.5 us (13%)
  matrix products  21.4 us (4%)
  starting transfers between devices  19.9 us (4%)
  between operations  14.6 us (3%)
  other arithmetic  10.6 us (2%)
    unnamed x2, waiting for transfers between devices  297 us
    ppermute x7, waiting for transfers between devices, from_behind_2(): return lax.ppermute(x, axis, [(i, (i + by) % size) for i in range(size)])  82.7 us
    unnamed x14, local copies, waits for them, and re-layouts  30.5 us
    dot_general x8, matrix products, stacked(): jnp.dot(tpl_block, scaled, preferred_element_type=jnp.float32)  21.4 us
    ppermute x7, starting transfers between devices, from_behind_2(): return lax.ppermute(x, axis, [(i, (i + by) % size) for i in range(size)])  18.7 us
    reshape x1, local copies, waits for them, and re-layouts, windows(): flat[..., :length * (span + 1)].reshape(leading + (length, span + 1))  11.9 us
    broadcast_in_dim x2, local copies, waits for them, and re-layouts, windows(): jnp.broadcast_to(extended[..., None, :], leading + (length + 1, span))  11.7 us
  transfers between devices with their start and end apart: 9, of which 8 were waited for; matrix products, arithmetic and copies ran while one was open for 17% of the time, Pallas kernels for 0%

commit v1 on v0

v1 whole, which is shorter than its diff:
```python
import jax
import jax.numpy as jnp
from jax import lax
from jax.experimental import pallas as pl
from jax.experimental.pallas import tpu as pltpu
from jax.sharding import PartitionSpec as P

MESH = pl.DeviceIdType.MESH
LAGS = 600
KPAD = 640
CHUNK = 896
UNITS = 8
PAIRS = 4
WIDE = 8320
ROWS = 8192


def kernel(
    tpl_ref, mask_ref, wav_ref, tail_ref, out_ref,
    wrecv, xs, hankel, invb, tf, lhs, own, exs, exr, us, ur, ds_, dr, fown, xsend, xrecv, osend,
    w_ss, w_rs, e_ss, e_rs, u_ss, u_rs, d_ss, d_rs, x_ss, x_rs, o_ss, o_rs,
):
    t = lax.axis_index("tm")
    s = lax.axis_index("sta")
    h = s // 16
    z = (s // 2) % 8
    c = s % 2
    sib = h * 16 + z * 2 + (1 - c)
    up = h * 16 + ((z + 1) % 8) * 2 + c
    down = h * 16 + ((z + 7) % 8) * 2 + c
    across = (1 - h) * 16 + z * 2 + c

    barrier = pltpu.get_barrier_semaphore()
    for step in range(1, UNITS):
        pl.semaphore_signal(barrier, inc=1, device_id=((t + step) % UNITS, s), device_id_type=MESH)
    for other in (sib, up, down, across):
        pl.semaphore_signal(barrier, inc=1, device_id=(t, other), device_id_type=MESH)
    pl.semaphore_wait(barrier, 11)

    def remote(src, dst, ssem, rsem, dev):
        return pltpu.make_async_remote_copy(
            src_ref=src, dst_ref=dst, send_sem=ssem, recv_sem=rsem, device_id=dev, device_id_type=MESH
        )

    wcopies = [
        remote(wav_ref, wrecv.at[k], w_ss.at[k], w_rs.at[k], ((t + k) % UNITS, s)) for k in range(1, UNITS)
    ]
    for cp in wcopies:
        cp.start()

    maskf = mask_ref[...].astype(jnp.float32)
    for comp in range(3):
        values = tpl_ref[comp].astype(jnp.float32)
        mean = jnp.sum(values, axis=0, keepdims=True) / LAGS
        centred = values - mean
        energy = jnp.sum(centred * centred, axis=0, keepdims=True)
        normed = centred * lax.rsqrt(energy + 1e-05) * maskf
        padded = jnp.concatenate([normed, jnp.zeros((KPAD - LAGS, 256), jnp.float32)], axis=0)
        tf[...] = padded.T
        for o in range(2):
            for d in range(8):
                zz = (z + d) % 8
                cc = c if o == 0 else 1 - c
                first = pl.multiple_of((h * 16 + zz * 2 + cc) * 8, 8)
                second = pl.multiple_of(((1 - h) * 16 + zz * 2 + cc) * 8, 8)
                both = jnp.concatenate([tf[pl.ds(first, 8), :], tf[pl.ds(second, 8), :]], axis=0)
                lhs[comp, 16 * (8 * o + d) : 16 * (8 * o + d) + 16, :] = both.astype(jnp.bfloat16)

    xs[...] = jnp.zeros((8, WIDE), jnp.float32)

    def place(value, start, width):
        v = value.astype(jnp.float32)
        xs[0:3, pl.ds(start, width)] = v
        xs[4:7, pl.ds(start, width)] = v * v

    place(wav_ref[...], pl.multiple_of(t * CHUNK, 128), CHUNK)
    place(tail_ref[...], 8 * CHUNK, LAGS - 1)
    for k in range(1, UNITS):
        wcopies[k - 1].wait_recv()
        place(wrecv[k], pl.multiple_of(((t + UNITS - k) % UNITS) * CHUNK, 128), CHUNK)

    def window(k, carry):
        at = pl.multiple_of(k * 1024, 128)
        a = xs[:, pl.ds(at, 1664)]

        def ahead(v, n):
            return pltpu.roll(v, 1664 - n, axis=1)

        sums = {1: a}
        n = 1
        while n < 512:
            sums[2 * n] = sums[n] + ahead(sums[n], n)
            n *= 2
        total = sums[512] + ahead(sums[64], 512) + ahead(sums[16], 576) + ahead(sums[8], 592)
        total = total[:, :1024]
        squares = pltpu.roll(total, 4, axis=0)
        inverse = lax.rsqrt(squares - total * total / LAGS + 1e-05)
        for comp in range(3):
            invb[comp, :, pl.ds(at, 1024)] = jnp.broadcast_to(inverse[comp : comp + 1], (8, 1024))
        return carry

    lax.fori_loop(0, 7, window, 0)

    sub = lax.broadcasted_iota(jnp.int32, (8, 640), 0)

    def skewed(k, carry):
        at = pl.multiple_of(k * 512, 128)
        for comp in range(3):
            v = jnp.broadcast_to(xs[comp : comp + 1, pl.ds(at, 640)], (8, 640))
            for bit in (1, 2, 4):
                v = jnp.where((sub & bit) != 0, pltpu.roll(v, 640 - bit, axis=1), v)
            for m in range(8):
                lo = v if m == 0 else pltpu.roll(v, 640 - 16 * m, axis=1)
                hi = pltpu.roll(v, 640 - 16 * m - 8, axis=1)
                both = jnp.concatenate([lo[:, :512], hi[:, :512]], axis=0).astype(jnp.bfloat16)
                for q in range(4):
                    hankel[comp, pl.ds(pl.multiple_of(at + 128 * q + 16 * m, 16), 16), :] = both[
                        :, 128 * q : 128 * q + 128
                    ]
        return carry

    lax.fori_loop(0, 16, skewed, 0)

    def compute(pair):
        def tile(i, carry):
            where = []
            for j in range(2):
                b = 2 * i + j
                second = (b >= 7).astype(jnp.int32)
                unit = 2 * pair + second
                inside = b - 7 * second
                q = (t + unit + 1) % UNITS
                where.append((unit, inside, pl.multiple_of(q * CHUNK + inside * 128, 128)))
            acc = None
            for comp in range(3):
                rhs = jnp.concatenate([hankel[comp, pl.ds(w[2], KPAD), :] for w in where], axis=1)
                prod = jnp.dot(lhs[comp], rhs, preferred_element_type=jnp.float32)
                inv = jnp.concatenate([invb[comp, :, pl.ds(w[2], 128)] for w in where], axis=1)
                prod = prod.reshape(32, 8, 256) * inv[None]
                acc = prod if acc is None else acc + prod
            acc = acc.reshape(256, 256)
            for j in range(2):
                unit, inside, _ = where[j]
                lanes = pl.ds(pl.multiple_of(inside * 128, 128), 128)
                own[unit, :, lanes] = acc[:128, 128 * j : 128 * j + 128]
                exs[unit, :, lanes] = acc[128:, 128 * j : 128 * j + 128].astype(jnp.bfloat16)
            return carry

        lax.fori_loop(0, 7, tile, 0)

    ecopies = [
        remote(exs.at[pl.ds(2 * p, 2)], exr.at[pl.ds(2 * p, 2)], e_ss.at[p], e_rs.at[p], (t, sib)) for p in range(PAIRS)
    ]
    ucopies = [
        [remote(us.at[u, k], ur.at[u, k], u_ss.at[u, k], u_rs.at[u, k], (t, up)) for k in range(4)] for u in range(UNITS)
    ]
    dcopies = [
        [remote(ds_.at[u, k], dr.at[u, k], d_ss.at[u, k], d_rs.at[u, k], (t, down)) for k in range(4)]
        for u in range(UNITS)
    ]
    xcopies = [remote(xsend.at[p], xrecv.at[p], x_ss.at[p], x_rs.at[p], (t, across)) for p in range(PAIRS)]
    ocopies = [
        remote(osend.at[u], out_ref.at[t], o_ss.at[u], o_rs.at[u], ((t + u + 1) % UNITS, s)) for u in range(UNITS - 1)
    ]
    started = []

    def begin(cp):
        cp.start()
        started.append(cp)

    def chunk(u, d):
        return own[u, 16 * d : 16 * d + 16, :] + exr[u, 16 * d : 16 * d + 16, :].astype(jnp.float32)

    def stage(pair, k):
        units = (2 * pair, 2 * pair + 1)
        if k == 1:
            ecopies[pair].wait_recv()
            us[units[0], 0] = chunk(units[0], 4).astype(jnp.bfloat16)
            begin(ucopies[units[0]][0])
            ds_[units[1], 0] = chunk(units[1], 4).astype(jnp.bfloat16)
            begin(dcopies[units[1]][0])
        elif k <= 4:
            for u in units:
                for copies, send, recv, d, first in (
                    (ucopies, us, ur, 5 - k, u % 2 == 0),
                    (dcopies, ds_, dr, 3 + k, u % 2 == 1),
                ):
                    v = chunk(u, d)
                    if k > 2 or first:
                        copies[u][k - 2].wait_recv()
                        v = v + recv[u, k - 2].astype(jnp.float32)
                    send[u, k - 1] = v.astype(jnp.bfloat16)
                    begin(copies[u][k - 1])
        elif k == 5:
            away = []
            for u in units:
                ucopies[u][3].wait_recv()
                dcopies[u][3].wait_recv()
                v = chunk(u, 0) + ur[u, 3].astype(jnp.float32) + dr[u, 3].astype(jnp.float32)
                fown[u] = v[:8]
                away.append(v[8:])
            xsend[pair] = jnp.concatenate(away, axis=0).astype(jnp.bfloat16)
            begin(xcopies[pair])
        else:
            xcopies[pair].wait_recv()
            got = xrecv[pair].astype(jnp.float32)
            for j, u in enumerate(units):
                v = fown[u] + got[8 * j : 8 * j + 8]
                if u < UNITS - 1:
                    osend[u] = v
                    begin(ocopies[u])
                else:
                    out_ref[t] = v

    for slot in range(PAIRS + 6):
        if slot < PAIRS:
            compute(slot)
            begin(ecopies[slot])
        for k in range(6, 0, -1):
            pair = slot - k
            if 0 <= pair < PAIRS:
                stage(pair, k)

    for u in range(UNITS - 1):
        remote(
            osend.at[u], out_ref.at[(t + UNITS - u - 1) % UNITS], o_ss.at[u], o_rs.at[u], ((t + u + 1) % UNITS, s)
        ).wait_recv()
    for cp in wcopies + started:
        cp.wait_send()


def per_device(templates, channel_mask, waveforms, waveform_tail):
    tpl = jnp.transpose(templates[0, :, 0], (1, 2, 0))
    mask = channel_mask.reshape(1, 256)
    bf, f32 = jnp.bfloat16, jnp.float32
    dma = pltpu.SemaphoreType.DMA
    vmem = pl.BlockSpec(memory_space=pltpu.VMEM)
    return pl.pallas_call(
        kernel,
        out_shape=jax.ShapeDtypeStruct((UNITS, 8, CHUNK), f32),
        in_specs=[vmem] * 4,
        out_specs=vmem,
        scratch_shapes=[
            pltpu.VMEM((UNITS, 3, CHUNK), bf),
            pltpu.VMEM((8, WIDE), f32),
            pltpu.VMEM((3, ROWS, 128), bf),
            pltpu.VMEM((3, 8, UNITS * CHUNK), f32),
            pltpu.VMEM((256, KPAD), f32),
            pltpu.VMEM((3, 256, KPAD), bf),
            pltpu.VMEM((UNITS, 128, CHUNK), f32),
            pltpu.VMEM((UNITS, 128, CHUNK), bf),
            pltpu.VMEM((UNITS, 128, CHUNK), bf),
            pltpu.VMEM((UNITS, 4, 16, CHUNK), bf),
            pltpu.VMEM((UNITS, 4, 16, CHUNK), bf),
            pltpu.VMEM((UNITS, 4, 16, CHUNK), bf),
            pltpu.VMEM((UNITS, 4, 16, CHUNK), bf),
            pltpu.VMEM((UNITS, 8, CHUNK), f32),
            pltpu.VMEM((PAIRS, 16, CHUNK), bf),
            pltpu.VMEM((PAIRS, 16, CHUNK), bf),
            pltpu.VMEM((UNITS, 8, CHUNK), f32),
            dma((UNITS,)), dma((UNITS,)),
            dma((PAIRS,)), dma((PAIRS,)),
            dma((UNITS, 4)), dma((UNITS, 4)),
            dma((UNITS, 4)), dma((UNITS, 4)),
            dma((PAIRS,)), dma((PAIRS,)),
            dma((UNITS,)), dma((UNITS,)),
        ],
        compiler_params=pltpu.CompilerParams(
            collective_id=0, has_side_effects=True, vmem_limit_bytes=50 * 1024 * 1024
        ),
    )(tpl, mask, waveforms[0], waveform_tail[0])


def solution(mesh):
    placed = (
        P("tm", None, "sta", None, None),
        P("tm", None, "sta"),
        P("sta", None, "tm"),
        P("sta", None, None),
    )
    return jax.shard_map(
        per_device, mesh=mesh, in_specs=placed, out_specs=P(None, "sta", "tm"), check_vma=False
    )
```

time: 523 us -> 70.3 us (0.13); the launches traced: 516 us -> 69.5 us
  waiting for transfers between devices: 381 us -> 0 us
  Pallas kernels: 0 us -> 65.6 us
  local copies, waits for them, and re-layouts: 68.5 us -> 3.93 us
  matrix products: 21.4 us -> 0 us
  starting transfers between devices: 19.9 us -> 0 us
  between operations: 14.6 us -> 0.01 us
  other arithmetic: 10.6 us -> 0 us
    unnamed x2 -> x0, waiting for transfers between devices: 297 us -> none
    ppermute x8 -> x0, waiting for transfers between devices: 84 us -> none  [the longest x7 82.7 us: from_behind_2(): return lax.ppermute(x, axis, [(i, (i + by) % size) for i in range(size)])]
    pallas_call x0 -> x1, Pallas kernels: none -> 65.6 us  [per_device(): pl.pallas_call(kernel, out_shape=jax.ShapeDtypeStruct((UNITS, 8, CHUNK),...]
    unnamed x14 -> x9, local copies, waits for them, and re-layouts: 30.5 us -> 3.93 us
    dot_general x8 -> x0, matrix products: 21.4 us -> none  [stacked(): jnp.dot(tpl_block, scaled, preferred_element_type=jnp.float32)]
    ppermute x8 -> x0, starting transfers between devices: 19.9 us -> none  [the longest x7 18.7 us: from_behind_2(): return lax.ppermute(x, axis, [(i, (i + by) % size) for i in range(size)])]
    reshape x2 -> x0, local copies, waits for them, and re-layouts: 11.9 us -> none  [the longest x1 11.9 us: windows(): flat[..., :length * (span + 1)].reshape(leading + (length, span + 1))]
    broadcast_in_dim x3 -> x0, local copies, waits for them, and re-layouts: 11.7 us -> none  [the longest x2 11.7 us: windows(): jnp.broadcast_to(extended[..., None, :], leading + (length + 1, span))]
  transfers between devices with their start and end apart: 9 -> 0, of which waited for: 8 -> 0; matrix products, arithmetic and copies ran while one was open for 17% -> 0% of each run, Pallas kernels for 0% -> 0%
where the time goes in v1:
time: 70.3 us; the launch traced here: 69.5 us
  Pallas kernels  65.6 us (93%)
  local copies, waits for them, and re-layouts  3.93 us (6%)
    pallas_call x1, Pallas kernels, per_device(): pl.pallas_call(kernel, out_shape=jax.ShapeDtypeStruct((UNITS, 8, CHUNK),...  65.6 us
    unnamed x9, local copies, waits for them, and re-layouts  3.93 us

profile of v1, /device:TPU:26, one launch (start us, length us, event | category | flops | bytes accessed | tf_op | source)
XLA Modules:
  0.0 69.5 jit_solution(9769629511944744146)
XLA Ops:
  0.0 0.0 copy-start.1
  0.0 0.7 copy-done.1
  0.7 0.0 copy-start
  0.7 1.2 %copy-done = bf16[1,256,1,3,600]{1,4,3,2,0:T(8,128)(2,1)S(1)} copy-done((bf16[1,256,1,3,600]{1,4,3,2,0:T(8,128)(2,1)S(1)}, bf16[1,256,1,3,600]{1,4,3,2,0:T(8,128)(2,1)}, u32[]{:S(2)}) %copy-start) | copy-done | bytes 921624
  1.9 0.0 copy-start.2
  1.9 0.7 copy-done.2
  2.6 0.0 copy-start.3
  2.6 0.7 copy-done.3
  3.2 65.6 %shard_map.46 = f32[8,8,896]{2,1,0:T(8,128)S(1)} custom-call(bf16[3,600,256]{2,1,0:T(8,128)(2,1)S(1)} %bitcast.6, s32[1,256]{1,0:T(1,128)S(1)} %bitcast.9, bf16[3,896]{1,0:T(4,128)(2,1)S(1)} %bitcast.7, bf16[3,599]{1,0:T(4,128)(2,1)S(1)} %bitcast.8), custom_call_target="tpu_custom_call" | custom-call | tf_op jit(solution)/shard_map/pallas_call | solution.py:238
  68.8 0.7 copy.6
Async XLA Ops:
  0.0 0.7 copy-start.1
  0.7 1.2 %copy-start = (bf16[1,256,1,3,600]{1,4,3,2,0:T(8,128)(2,1)S(1)}, bf16[1,256,1,3,600]{1,4,3,2,0:T(8,128)(2,1)}, u32[]{:S(2)}) copy-start(bf16[1,256,1,3,600]{1,4,3,2,0:T(8,128)(2,1)} %param.4) | copy-start | bytes 2764804
  1.9 0.7 copy-start.2
  2.6 0.7 copy-start.3

commit v2 on v0

v2 whole, which is shorter than its diff:
```python
import jax
import jax.numpy as jnp
from jax import lax
from jax.experimental import pallas as pl
from jax.experimental.pallas import tpu as pltpu
from jax.sharding import PartitionSpec as P

MESH = pl.DeviceIdType.MESH
LAGS = 600
KPAD = 640
CHUNK = 896
UNITS = 8
TILES = 28
WIDE = 7936
BLOCKS = 60
TILE_US, EXCHANGE_US, HOP_US, QUEUE_US = 0.35, 1.0, 3.2, 0.2


def order_of_work():
    events = [(TILE_US * i, 0, ("tile", i)) for i in range(TILES)]
    for u in range(UNITS):
        done = TILE_US * (7 * (u // 2) + (4 if u % 2 == 0 else 7))
        for k in range(1, 6):
            when = done + EXCHANGE_US + HOP_US * (k - 1) + QUEUE_US * u * (k > 1)
            events.append((when, 1, ("stage", u, k)))
    return [e[2] for e in sorted(events, key=lambda e: (e[0], e[1], -e[2][-1]))]


def kernel(
    tpl_hbm, mask_hbm, wav_hbm, tail_hbm, out_ref,
    tpl_ref, mask_ref, wav_ref, tail_ref, wrecv, xs, hankel, invb, tf, lhs, own, exs, exr, us, ur, ds_, dr,
    fsend, frecv,
    l_sem, w_ss, w_rs, e_ss, e_rs, u_ss, u_rs, d_ss, d_rs, f_ss, f_rs,
):
    t = lax.axis_index("tm")
    s = lax.axis_index("sta")
    h = s // 16
    z = (s // 2) % 8
    c = s % 2
    sib = h * 16 + z * 2 + (1 - c)
    up = h * 16 + ((z + 1) % 8) * 2 + c
    down = h * 16 + ((z + 7) % 8) * 2 + c
    across = (1 - h) * 16 + z * 2 + c

    locals_ = [
        pltpu.make_async_copy(src, dst, l_sem.at[i])
        for i, (src, dst) in enumerate(
            ((wav_hbm, wav_ref), (tail_hbm, tail_ref), (mask_hbm, mask_ref), (tpl_hbm, tpl_ref))
        )
    ]
    for cp in locals_:
        cp.start()
    barrier = pltpu.get_barrier_semaphore()
    for step in range(1, UNITS):
        pl.semaphore_signal(barrier, inc=1, device_id=((t + step) % UNITS, s), device_id_type=MESH)
    for step in range(UNITS):
        pl.semaphore_signal(barrier, inc=1, device_id=((t + step) % UNITS, across), device_id_type=MESH)
    for other in (sib, up, down):
        pl.semaphore_signal(barrier, inc=1, device_id=(t, other), device_id_type=MESH)
    xs[...] = jnp.zeros((8, WIDE), jnp.float32)
    for cp in locals_:
        cp.wait()

    maskf = mask_ref[...].astype(jnp.float32)

    def templates(comp):
        values = tpl_ref[comp].astype(jnp.float32)
        mean = jnp.sum(values, axis=0, keepdims=True) / LAGS
        centred = values - mean
        energy = jnp.sum(centred * centred, axis=0, keepdims=True)
        normed = centred * lax.rsqrt(energy + 1e-05) * maskf
        padded = jnp.concatenate([normed, jnp.zeros((KPAD - LAGS, 256), jnp.float32)], axis=0)
        tf[comp] = padded.T
        for o in range(2):
            for d in range(8):
                zz = (z + d) % 8
                cc = c if o == 0 else 1 - c
                first = pl.multiple_of((h * 16 + zz * 2 + cc) * 8, 8)
                second = pl.multiple_of(((1 - h) * 16 + zz * 2 + cc) * 8, 8)
                both = jnp.concatenate([tf[comp, pl.ds(first, 8), :], tf[comp, pl.ds(second, 8), :]], axis=0)
                lhs[comp, 16 * (8 * o + d) : 16 * (8 * o + d) + 16, :] = both.astype(jnp.bfloat16)

    def place(value, start, width):
        v = value.astype(jnp.float32)
        xs[0:3, pl.ds(start, width)] = v
        xs[4:7, pl.ds(start, width)] = v * v

    templates(0)
    pl.semaphore_wait(barrier, 18)

    def remote(src, dst, ssem, rsem, dev):
        return pltpu.make_async_remote_copy(
            src_ref=src, dst_ref=dst, send_sem=ssem, recv_sem=rsem, device_id=dev, device_id_type=MESH
        )

    started = []

    def begin(cp):
        cp.start()
        started.append(cp)

    wcopies = [
        remote(wav_ref, wrecv.at[k], w_ss.at[k], w_rs.at[k], ((t + k) % UNITS, s)) for k in range(1, UNITS)
    ]
    for cp in wcopies:
        begin(cp)
    templates(1)
    templates(2)
    place(wav_ref[...], pl.multiple_of(t * CHUNK, 128), CHUNK)
    place(tail_ref[...], 8 * CHUNK, LAGS - 1)
    for k in range(1, UNITS):
        wcopies[k - 1].wait_recv()
        place(wrecv[k], pl.multiple_of(((t + UNITS - k) % UNITS) * CHUNK, 128), CHUNK)

    def window(at):
        a = xs[:, at : at + 1664]

        def ahead(v, n):
            return pltpu.roll(v, 1664 - n, axis=1)

        sums = {1: a}
        n = 1
        while n < 512:
            sums[2 * n] = sums[n] + ahead(sums[n], n)
            n *= 2
        total = sums[512] + ahead(sums[64], 512) + ahead(sums[16], 576) + ahead(sums[8], 592)
        total = total[:, :1024]
        squares = pltpu.roll(total, 4, axis=0)
        inverse = lax.rsqrt(squares - total * total / LAGS + 1e-05)
        for comp in range(3):
            invb[comp, :, at : at + 1024] = jnp.broadcast_to(inverse[comp : comp + 1], (8, 1024))

    def prepare(first, blocks):
        width = 128 * (blocks + 1)
        sub = lax.broadcasted_iota(jnp.int32, (8, width), 0)
        at = 128 * first
        for comp in range(3):
            v = jnp.broadcast_to(xs[comp : comp + 1, at : at + width], (8, width))
            for bit in (1, 2, 4):
                v = jnp.where((sub & bit) != 0, pltpu.roll(v, width - bit, axis=1), v)
            v = jnp.concatenate([v, pltpu.roll(v, width - 8, axis=1)], axis=0).astype(jnp.bfloat16)
            for m in range(8):
                both = v if m == 0 else pltpu.roll(v, width - 16 * m, axis=1)
                for q in range(blocks):
                    hankel[comp, at + 128 * q + 16 * m : at + 128 * q + 16 * m + 16, :] = both[
                        :, 128 * q : 128 * q + 128
                    ]

    origin = (s // 32) * 128

    def tile(i):
        at = pl.multiple_of(origin + 256 * i, 128)
        acc = None
        for comp in range(3):
            rhs = jnp.concatenate(
                [hankel[comp, pl.ds(pl.multiple_of(at + 128 * j, 128), KPAD), :] for j in range(2)], axis=1
            )
            prod = jnp.dot(lhs[comp], rhs, preferred_element_type=jnp.float32)
            prod = prod.reshape(32, 8, 256) * invb[comp, :, pl.ds(at, 256)][None]
            acc = prod if acc is None else acc + prod
        acc = acc.reshape(256, 256)
        for j in range(2):
            u, inside = divmod(2 * i + j, 7)
            own[u, :, 128 * inside : 128 * inside + 128] = acc[:128, 128 * j : 128 * j + 128]
            exs[u, :, 128 * inside : 128 * inside + 128] = acc[128:, 128 * j : 128 * j + 128].astype(jnp.bfloat16)
        if i % 7 in (3, 6):
            begin(exchange((2 * i + 1) // 7 - (1 if i % 7 == 3 else 0)))

    def exchange(u):
        return remote(exs.at[u], exr.at[u], e_ss.at[u], e_rs.at[u], (t, sib))

    def upward(u, k):
        return remote(us.at[u, k], ur.at[u, k], u_ss.at[u, k], u_rs.at[u, k], (t, up))

    def downward(u, k):
        return remote(ds_.at[u, k], dr.at[u, k], d_ss.at[u, k], d_rs.at[u, k], (t, down))

    def chunk(u, d):
        return own[u, 16 * d : 16 * d + 16, :] + exr[u, 16 * d : 16 * d + 16, :].astype(jnp.float32)

    def final(e, u, owner):
        return remote(
            fsend.at[e, u], frecv.at[e, t], f_ss.at[e, u], f_rs.at[e, t], (owner, s if e == 0 else across)
        )

    def stage(u, k):
        long_up = u % 2 == 0
        ways = (
            (upward, us, ur, 4 if long_up else 3, -1),
            (downward, ds_, dr, 3 if long_up else 4, 1),
        )
        if k == 1:
            exchange(u).wait_recv()
        if k <= 4:
            for way, send, recv, hops, sign in ways:
                if k <= hops:
                    left = hops - k + 1
                    v = chunk(u, left if sign < 0 else 8 - left)
                    if k > 1:
                        way(u, k - 2).wait_recv()
                        v = v + recv[u, k - 2].astype(jnp.float32)
                    send[u, k - 1] = v.astype(jnp.bfloat16)
                    begin(way(u, k - 1))
        else:
            v = chunk(u, 0)
            for way, send, recv, hops, sign in ways:
                way(u, hops - 1).wait_recv()
                v = v + recv[u, hops - 1].astype(jnp.float32)
            fsend[0, u] = v[:8]
            fsend[1, u] = v[8:]

            @pl.when(t != u)
            def _():
                final(0, u, u).start()

            @pl.when(t == u)
            def _():
                frecv[0, u] = v[:8]

            final(1, u, u).start()

    for k in range(7):
        window(1024 * k)
    prepare(0, BLOCKS)
    for what in order_of_work():
        if what[0] == "tile":
            tile(what[1])
        else:
            stage(what[1], what[2])

    for u in range(UNITS):
        def arrival(e, u=u):
            return remote(fsend.at[e, u], frecv.at[e, u], f_ss.at[e, u], f_rs.at[e, u], (u, s if e == 0 else across))

        @pl.when(t != u)
        def _():
            arrival(0).wait()

        arrival(1).wait()
        out_ref[u] = frecv[0, u] + frecv[1, u]
    for cp in started:
        cp.wait_send()


def per_device(templates, channel_mask, waveforms, waveform_tail):
    tpl = jnp.transpose(templates[0, :, 0], (1, 2, 0))
    mask = channel_mask.reshape(1, 256)
    bf, f32 = jnp.bfloat16, jnp.float32
    dma = pltpu.SemaphoreType.DMA
    anywhere = pl.BlockSpec(memory_space=pl.ANY)
    return pl.pallas_call(
        kernel,
        out_shape=jax.ShapeDtypeStruct((UNITS, 8, CHUNK), f32),
        in_specs=[anywhere] * 4,
        out_specs=pl.BlockSpec(memory_space=pltpu.VMEM),
        scratch_shapes=[
            pltpu.VMEM((3, LAGS, 256), bf),
            pltpu.VMEM((1, 256), jnp.int32),
            pltpu.VMEM((3, CHUNK), bf),
            pltpu.VMEM((3, LAGS - 1), bf),
            pltpu.VMEM((UNITS, 3, CHUNK), bf),
            pltpu.VMEM((8, WIDE), f32),
            pltpu.VMEM((3, 128 * BLOCKS, 128), bf),
            pltpu.VMEM((3, 8, UNITS * CHUNK), f32),
            pltpu.VMEM((3, 256, KPAD), f32),
            pltpu.VMEM((3, 256, KPAD), bf),
            pltpu.VMEM((UNITS, 128, CHUNK), f32),
            pltpu.VMEM((UNITS, 128, CHUNK), bf),
            pltpu.VMEM((UNITS, 128, CHUNK), bf),
            pltpu.VMEM((UNITS, 4, 16, CHUNK), bf),
            pltpu.VMEM((UNITS, 4, 16, CHUNK), bf),
            pltpu.VMEM((UNITS, 4, 16, CHUNK), bf),
            pltpu.VMEM((UNITS, 4, 16, CHUNK), bf),
            pltpu.VMEM((2, UNITS, 8, CHUNK), f32),
            pltpu.VMEM((2, UNITS, 8, CHUNK), f32),
            dma((4,)),
            dma((UNITS,)), dma((UNITS,)),
            dma((UNITS,)), dma((UNITS,)),
            dma((UNITS, 4)), dma((UNITS, 4)),
            dma((UNITS, 4)), dma((UNITS, 4)),
            dma((2, UNITS)), dma((2, UNITS)),
        ],
        compiler_params=pltpu.CompilerParams(
            collective_id=0, has_side_effects=True, vmem_limit_bytes=50 * 1024 * 1024
        ),
    )(tpl, mask, waveforms[0], waveform_tail[0])


def solution(mesh):
    placed = (
        P("tm", None, "sta", None, None),
        P("tm", None, "sta"),
        P("sta", None, "tm"),
        P("sta", None, None),
    )
    return jax.shard_map(
        per_device, mesh=mesh, in_specs=placed, out_specs=P(None, "sta", "tm"), check_vma=False
    )
```

time: 523 us -> 54 us (0.10); the launches traced: 516 us -> 53.8 us
  waiting for transfers between devices: 381 us -> 0 us
  local copies, waits for them, and re-layouts: 68.5 us -> 3.93 us
  Pallas kernels: 0 us -> 49.9 us
  matrix products: 21.4 us -> 0 us
  starting transfers between devices: 19.9 us -> 0 us
  between operations: 14.6 us -> 0.01 us
  other arithmetic: 10.6 us -> 0 us
    unnamed x2 -> x0, waiting for transfers between devices: 297 us -> none
    ppermute x8 -> x0, waiting for transfers between devices: 84 us -> none  [the longest x7 82.7 us: from_behind_2(): return lax.ppermute(x, axis, [(i, (i + by) % size) for i in range(size)])]
    pallas_call x0 -> x1, Pallas kernels: none -> 49.9 us  [per_device(): pl.pallas_call(kernel, out_shape=jax.ShapeDtypeStruct((UNITS, 8, CHUNK),...]
    unnamed x14 -> x9, local copies, waits for them, and re-layouts: 30.5 us -> 3.93 us
    dot_general x8 -> x0, matrix products: 21.4 us -> none  [stacked(): jnp.dot(tpl_block, scaled, preferred_element_type=jnp.float32)]
    ppermute x8 -> x0, starting transfers between devices: 19.9 us -> none  [the longest x7 18.7 us: from_behind_2(): return lax.ppermute(x, axis, [(i, (i + by) % size) for i in range(size)])]
    reshape x2 -> x0, local copies, waits for them, and re-layouts: 11.9 us -> none  [the longest x1 11.9 us: windows(): flat[..., :length * (span + 1)].reshape(leading + (length, span + 1))]
    broadcast_in_dim x3 -> x0, local copies, waits for them, and re-layouts: 11.7 us -> none  [the longest x2 11.7 us: windows(): jnp.broadcast_to(extended[..., None, :], leading + (length + 1, span))]
  transfers between devices with their start and end apart: 9 -> 0, of which waited for: 8 -> 0; matrix products, arithmetic and copies ran while one was open for 17% -> 0% of each run, Pallas kernels for 0% -> 0%
where the time goes in v2:
time: 54 us; the launch traced here: 53.8 us
  Pallas kernels  49.9 us (92%)
  local copies, waits for them, and re-layouts  3.93 us (7%)
    pallas_call x1, Pallas kernels, per_device(): pl.pallas_call(kernel, out_shape=jax.ShapeDtypeStruct((UNITS, 8, CHUNK),...  49.9 us
    unnamed x9, local copies, waits for them, and re-layouts  3.93 us

profile of v2, /device:TPU:26, one launch (start us, length us, event | category | flops | bytes accessed | tf_op | source)
XLA Modules:
  0.0 53.8 jit_solution(4135767360219143672)
XLA Ops:
  0.0 0.0 copy-start.1
  0.0 0.7 %copy-done.1 = bf16[1,3,896]{2,1,0:T(4,128)(2,1)S(1)} copy-done((bf16[1,3,896]{2,1,0:T(4,128)(2,1)S(1)}, bf16[1,3,896]{2,1,0:T(4,128)(2,1)}, u32[]{:S(2)}) %copy-start.1) | copy-done | bytes 5400
  0.7 0.0 copy-start
  0.7 1.2 %copy-done = bf16[1,256,1,3,600]{1,4,3,2,0:T(8,128)(2,1)S(1)} copy-done((bf16[1,256,1,3,600]{1,4,3,2,0:T(8,128)(2,1)S(1)}, bf16[1,256,1,3,600]{1,4,3,2,0:T(8,128)(2,1)}, u32[]{:S(2)}) %copy-start) | copy-done | bytes 921624
  1.9 0.0 copy-start.2
  1.9 0.7 %copy-done.2 = bf16[1,3,599]{2,1,0:T(4,128)(2,1)S(1)} copy-done((bf16[1,3,599]{2,1,0:T(4,128)(2,1)S(1)}, bf16[1,3,599]{2,1,0:T(4,128)(2,1)}, u32[]{:S(2)}) %copy-start.2) | copy-done | bytes 3618
  2.6 0.0 copy-start.3
  2.6 0.7 %copy-done.3 = s32[1,256,1]{1,2,0:T(1,128)S(1)} copy-done((s32[1,256,1]{1,2,0:T(1,128)S(1)}, s32[1,256,1]{1,2,0:T(1,128)}, u32[]{:S(2)}) %copy-start.3) | copy-done | bytes 1048
  3.2 49.9 %shard_map.46 = f32[8,8,896]{2,1,0:T(8,128)S(1)} custom-call(bf16[3,600,256]{2,1,0:T(8,128)(2,1)S(1)} %bitcast.6, s32[1,256]{1,0:T(1,128)S(1)} %bitcast.9, bf16[3,896]{1,0:T(4,128)(2,1)S(1)} %bitcast.7, bf16[3,599]{1,0:T(4,128)(2,1)S(1)} %bitcast.8), custom_call_target="tpu_custom_call" | custom-call | tf_op jit(solution)/shard_map/pallas_call | solution.py:251
  53.1 0.7 %copy.6 = f32[8,8,896]{2,1,0:T(8,128)} copy(f32[8,8,896]{2,1,0:T(8,128)S(1)} %shard_map.46) | data formatting | bytes 458752
Async XLA Ops:
  0.0 0.7 %copy-start.1 = (bf16[1,3,896]{2,1,0:T(4,128)(2,1)S(1)}, bf16[1,3,896]{2,1,0:T(4,128)(2,1)}, u32[]{:S(2)}) copy-start(bf16[1,3,896]{2,1,0:T(4,128)(2,1)} %param.6) | copy-start | bytes 16132
  0.7 1.2 %copy-start = (bf16[1,256,1,3,600]{1,4,3,2,0:T(8,128)(2,1)S(1)}, bf16[1,256,1,3,600]{1,4,3,2,0:T(8,128)(2,1)}, u32[]{:S(2)}) copy-start(bf16[1,256,1,3,600]{1,4,3,2,0:T(8,128)(2,1)} %param.4) | copy-start | bytes 2764804
  1.9 0.7 %copy-start.2 = (bf16[1,3,599]{2,1,0:T(4,128)(2,1)S(1)}, bf16[1,3,599]{2,1,0:T(4,128)(2,1)}, u32[]{:S(2)}) copy-start(bf16[1,3,599]{2,1,0:T(4,128)(2,1)} %param.7) | copy-start | bytes 10786
  2.6 0.7 %copy-start.3 = (s32[1,256,1]{1,2,0:T(1,128)S(1)}, s32[1,256,1]{1,2,0:T(1,128)}, u32[]{:S(2)}) copy-start(s32[1,256,1]{1,2,0:T(1,128)} %param.5) | copy-start | bytes 3076

commit v3 on v2

--- a/solution.py
+++ b/solution.py
@@ -13,7 +13,7 @@
 TILES = 28
 WIDE = 7936
 BLOCKS = 60
-TILE_US, EXCHANGE_US, HOP_US, QUEUE_US = 0.35, 1.0, 3.2, 0.2
+TILE_US, EXCHANGE_US, HOP_US, QUEUE_US = 0.35, 1.5, 3.2, 0.0
 
 
 def order_of_work():
@@ -93,14 +93,11 @@
             src_ref=src, dst_ref=dst, send_sem=ssem, recv_sem=rsem, device_id=dev, device_id_type=MESH
         )
 
-    started = []
-
     def begin(cp):
         cp.start()
-        started.append(cp)
 
     wcopies = [
-        remote(wav_ref, wrecv.at[k], w_ss.at[k], w_rs.at[k], ((t + k) % UNITS, s)) for k in range(1, UNITS)
+        remote(wav_ref, wrecv.at[k], w_ss, w_rs.at[k], ((t + k) % UNITS, s)) for k in range(1, UNITS)
     ]
     for cp in wcopies:
         begin(cp)
@@ -162,52 +159,60 @@
         for j in range(2):
             u, inside = divmod(2 * i + j, 7)
             own[u, :, 128 * inside : 128 * inside + 128] = acc[:128, 128 * j : 128 * j + 128]
-            exs[u, :, 128 * inside : 128 * inside + 128] = acc[128:, 128 * j : 128 * j + 128].astype(jnp.bfloat16)
+            exs[u, :, 128 * inside : 128 * inside + 128] = acc[128:, 128 * j : 128 * j + 128]
         if i % 7 in (3, 6):
             begin(exchange((2 * i + 1) // 7 - (1 if i % 7 == 3 else 0)))
 
     def exchange(u):
-        return remote(exs.at[u], exr.at[u], e_ss.at[u], e_rs.at[u], (t, sib))
+        return remote(exs.at[u], exr.at[u], e_ss, e_rs.at[u], (t, sib))
+
+    def up_slot(u, k):
+        return 7 * (u // 2) + 4 * (u % 2) + k
+
+    def down_slot(u, k):
+        return 7 * (u // 2) + 3 * (u % 2) + k
 
     def upward(u, k):
-        return remote(us.at[u, k], ur.at[u, k], u_ss.at[u, k], u_rs.at[u, k], (t, up))
+        i = up_slot(u, k)
+        return remote(us.at[i], ur.at[i], u_ss, u_rs.at[i], (t, up))
 
     def downward(u, k):
-        return remote(ds_.at[u, k], dr.at[u, k], d_ss.at[u, k], d_rs.at[u, k], (t, down))
+        i = down_slot(u, k)
+        return remote(ds_.at[i], dr.at[i], d_ss, d_rs.at[i], (t, down))
 
     def chunk(u, d):
-        return own[u, 16 * d : 16 * d + 16, :] + exr[u, 16 * d : 16 * d + 16, :].astype(jnp.float32)
+        return own[u, 16 * d : 16 * d + 16, :] + exr[u, 16 * d : 16 * d + 16, :]
 
     def final(e, u, owner):
         return remote(
-            fsend.at[e, u], frecv.at[e, t], f_ss.at[e, u], f_rs.at[e, t], (owner, s if e == 0 else across)
+            fsend.at[e, u], frecv.at[e, t], f_ss.at[e], f_rs.at[e, t], (owner, s if e == 0 else across)
         )
 
     def stage(u, k):
         long_up = u % 2 == 0
         ways = (
-            (upward, us, ur, 4 if long_up else 3, -1),
-            (downward, ds_, dr, 3 if long_up else 4, 1),
+            (upward, up_slot, us, ur, 4 if long_up else 3, -1),
+            (downward, down_slot, ds_, dr, 3 if long_up else 4, 1),
         )
         if k == 1:
             exchange(u).wait_recv()
         if k <= 4:
-            for way, send, recv, hops, sign in ways:
+            for way, slot, send, recv, hops, sign in ways:
                 if k <= hops:
                     left = hops - k + 1
                     v = chunk(u, left if sign < 0 else 8 - left)
                     if k > 1:
                         way(u, k - 2).wait_recv()
-                        v = v + recv[u, k - 2].astype(jnp.float32)
-                    send[u, k - 1] = v.astype(jnp.bfloat16)
+                        v = v + recv[slot(u, k - 2)].astype(jnp.float32)
+                    send[slot(u, k - 1)] = v.astype(jnp.bfloat16)
                     begin(way(u, k - 1))
         else:
             v = chunk(u, 0)
-            for way, send, recv, hops, sign in ways:
+            for way, slot, send, recv, hops, sign in ways:
                 way(u, hops - 1).wait_recv()
-                v = v + recv[u, hops - 1].astype(jnp.float32)
-            fsend[0, u] = v[:8]
-            fsend[1, u] = v[8:]
+                v = v + recv[slot(u, hops - 1)].astype(jnp.float32)
+            fsend[0, u] = v[:8].astype(jnp.bfloat16)
+            fsend[1, u] = v[8:].astype(jnp.bfloat16)
 
             @pl.when(t != u)
             def _():
@@ -215,7 +220,7 @@
 
             @pl.when(t == u)
             def _():
-                frecv[0, u] = v[:8]
+                frecv[0, u] = v[:8].astype(jnp.bfloat16)
 
             final(1, u, u).start()
 
@@ -225,21 +230,30 @@
     for what in order_of_work():
         if what[0] == "tile":
             tile(what[1])
+            if what[1] == 3:
+                pass
         else:
             stage(what[1], what[2])
 
     for u in range(UNITS):
         def arrival(e, u=u):
-            return remote(fsend.at[e, u], frecv.at[e, u], f_ss.at[e, u], f_rs.at[e, u], (u, s if e == 0 else across))
+            return remote(fsend.at[e, u], frecv.at[e, u], f_ss.at[e], f_rs.at[e, u], (u, s if e == 0 else across))
 
         @pl.when(t != u)
         def _():
-            arrival(0).wait()
-
-        arrival(1).wait()
-        out_ref[u] = frecv[0, u] + frecv[1, u]
-    for cp in started:
-        cp.wait_send()
+            arrival(0).wait_recv()
+
+        arrival(1).wait_recv()
+        out_ref[u] = frecv[0, u].astype(jnp.float32) + frecv[1, u].astype(jnp.float32)
+    for sent, sem in (
+        (wrecv.at[pl.ds(1, UNITS - 1)], w_ss),
+        (exs, e_ss),
+        (us, u_ss),
+        (ds_, d_ss),
+        (fsend.at[0, pl.ds(1, UNITS - 1)], f_ss.at[0]),
+        (fsend.at[1], f_ss.at[1]),
+    ):
+        remote(sent, sent, sem, w_rs.at[0], (t, sib)).wait_send()
 
 
 def per_device(templates, channel_mask, waveforms, waveform_tail):
@@ -265,20 +279,20 @@
             pltpu.VMEM((3, 256, KPAD), f32),
             pltpu.VMEM((3, 256, KPAD), bf),
             pltpu.VMEM((UNITS, 128, CHUNK), f32),
-            pltpu.VMEM((UNITS, 128, CHUNK), bf),
-            pltpu.VMEM((UNITS, 128, CHUNK), bf),
-            pltpu.VMEM((UNITS, 4, 16, CHUNK), bf),
-            pltpu.VMEM((UNITS, 4, 16, CHUNK), bf),
-            pltpu.VMEM((UNITS, 4, 16, CHUNK), bf),
-            pltpu.VMEM((UNITS, 4, 16, CHUNK), bf),
-            pltpu.VMEM((2, UNITS, 8, CHUNK), f32),
-            pltpu.VMEM((2, UNITS, 8, CHUNK), f32),
+            pltpu.VMEM((UNITS, 128, CHUNK), f32),
+            pltpu.VMEM((UNITS, 128, CHUNK), f32),
+            pltpu.VMEM((28, 16, CHUNK), bf),
+            pltpu.VMEM((28, 16, CHUNK), bf),
+            pltpu.VMEM((28, 16, CHUNK), bf),
+            pltpu.VMEM((28, 16, CHUNK), bf),
+            pltpu.VMEM((2, UNITS, 8, CHUNK), bf),
+            pltpu.VMEM((2, UNITS, 8, CHUNK), bf),
             dma((4,)),
-            dma((UNITS,)), dma((UNITS,)),
-            dma((UNITS,)), dma((UNITS,)),
-            dma((UNITS, 4)), dma((UNITS, 4)),
-            dma((UNITS, 4)), dma((UNITS, 4)),
-            dma((2, UNITS)), dma((2, UNITS)),
+            dma, dma((UNITS,)),
+            dma, dma((UNITS,)),
+            dma, dma((28,)),
+            dma, dma((28,)),
+            dma((2,)), dma((2, UNITS)),
         ],
         compiler_params=pltpu.CompilerParams(
             collective_id=0, has_side_effects=True, vmem_limit_bytes=50 * 1024 * 1024

time: 54 us -> 50.9 us (0.943)
  Pallas kernels: 49.9 us -> 46.8 us
    pallas_call x1, Pallas kernels: 49.9 us -> 46.8 us  [per_device(): pl.pallas_call(kernel, out_shape=jax.ShapeDtypeStruct((UNITS, 8, CHUNK),...]
where the time goes in v3:
time: 50.9 us; the launch traced here: 50.7 us
  Pallas kernels  46.8 us (92%)
  local copies, waits for them, and re-layouts  3.93 us (8%)
    pallas_call x1, Pallas kernels, per_device(): pl.pallas_call(kernel, out_shape=jax.ShapeDtypeStruct((UNITS, 8, CHUNK),...  46.8 us
    unnamed x9, local copies, waits for them, and re-layouts  3.93 us

profile of v3, /device:TPU:26, one launch (start us, length us, event | category | flops | bytes accessed | tf_op | source)
XLA Modules:
  0.0 50.7 jit_solution(9599923309303951630)
XLA Ops:
  0.0 0.0 copy-start.1
  0.0 0.7 %copy-done.1 = bf16[1,3,896]{2,1,0:T(4,128)(2,1)S(1)} copy-done((bf16[1,3,896]{2,1,0:T(4,128)(2,1)S(1)}, bf16[1,3,896]{2,1,0:T(4,128)(2,1)}, u32[]{:S(2)}) %copy-start.1) | copy-done | bytes 5400
  0.7 0.0 copy-start
  0.7 1.2 %copy-done = bf16[1,256,1,3,600]{1,4,3,2,0:T(8,128)(2,1)S(1)} copy-done((bf16[1,256,1,3,600]{1,4,3,2,0:T(8,128)(2,1)S(1)}, bf16[1,256,1,3,600]{1,4,3,2,0:T(8,128)(2,1)}, u32[]{:S(2)}) %copy-start) | copy-done | bytes 921624
  1.9 0.0 copy-start.2
  1.9 0.7 %copy-done.2 = bf16[1,3,599]{2,1,0:T(4,128)(2,1)S(1)} copy-done((bf16[1,3,599]{2,1,0:T(4,128)(2,1)S(1)}, bf16[1,3,599]{2,1,0:T(4,128)(2,1)}, u32[]{:S(2)}) %copy-start.2) | copy-done | bytes 3618
  2.6 0.0 copy-start.3
  2.6 0.7 %copy-done.3 = s32[1,256,1]{1,2,0:T(1,128)S(1)} copy-done((s32[1,256,1]{1,2,0:T(1,128)S(1)}, s32[1,256,1]{1,2,0:T(1,128)}, u32[]{:S(2)}) %copy-start.3) | copy-done | bytes 1048
  3.2 46.8 %shard_map.46 = f32[8,8,896]{2,1,0:T(8,128)S(1)} custom-call(bf16[3,600,256]{2,1,0:T(8,128)(2,1)S(1)} %bitcast.6, s32[1,256]{1,0:T(1,128)S(1)} %bitcast.9, bf16[3,896]{1,0:T(4,128)(2,1)S(1)} %bitcast.7, bf16[3,599]{1,0:T(4,128)(2,1)S(1)} %bitcast.8), custom_call_target="tpu_custom_call" | custom-call | tf_op jit(solution)/shard_map/pallas_call | solution.py:265
  50.0 0.7 %copy.6 = f32[8,8,896]{2,1,0:T(8,128)} copy(f32[8,8,896]{2,1,0:T(8,128)S(1)} %shard_map.46) | data formatting | bytes 458752
Async XLA Ops:
  0.0 0.7 %copy-start.1 = (bf16[1,3,896]{2,1,0:T(4,128)(2,1)S(1)}, bf16[1,3,896]{2,1,0:T(4,128)(2,1)}, u32[]{:S(2)}) copy-start(bf16[1,3,896]{2,1,0:T(4,128)(2,1)} %param.6) | copy-start | bytes 16132
  0.7 1.2 %copy-start = (bf16[1,256,1,3,600]{1,4,3,2,0:T(8,128)(2,1)S(1)}, bf16[1,256,1,3,600]{1,4,3,2,0:T(8,128)(2,1)}, u32[]{:S(2)}) copy-start(bf16[1,256,1,3,600]{1,4,3,2,0:T(8,128)(2,1)} %param.4) | copy-start | bytes 2764804
  1.9 0.7 %copy-start.2 = (bf16[1,3,599]{2,1,0:T(4,128)(2,1)S(1)}, bf16[1,3,599]{2,1,0:T(4,128)(2,1)}, u32[]{:S(2)}) copy-start(bf16[1,3,599]{2,1,0:T(4,128)(2,1)} %param.7) | copy-start | bytes 10786
  2.6 0.7 %copy-start.3 = (s32[1,256,1]{1,2,0:T(1,128)S(1)}, s32[1,256,1]{1,2,0:T(1,128)}, u32[]{:S(2)}) copy-start(s32[1,256,1]{1,2,0:T(1,128)} %param.5) | copy-start | bytes 3076

commit v4 on v3

--- a/solution.py
+++ b/solution.py
@@ -295,7 +295,7 @@
             dma((2,)), dma((2, UNITS)),
         ],
         compiler_params=pltpu.CompilerParams(
-            collective_id=0, has_side_effects=True, vmem_limit_bytes=50 * 1024 * 1024
+            collective_id=0, has_side_effects=True
         ),
     )(tpl, mask, waveforms[0], waveform_tail[0])
 

time: 50.9 us -> 49 us (0.963)
  local copies, waits for them, and re-layouts: 3.93 us -> 1.64 us
    unnamed x9 -> x1, local copies, waits for them, and re-layouts: 3.93 us -> 1.64 us
where the time goes in v4:
time: 49 us; the launch traced here: 48.8 us
  Pallas kernels  47.2 us (96%)
  local copies, waits for them, and re-layouts  1.64 us (3%)
    pallas_call x1, Pallas kernels, per_device(): pl.pallas_call(kernel, out_shape=jax.ShapeDtypeStruct((UNITS, 8, CHUNK),...  47.2 us
    unnamed x1, local copies, waits for them, and re-layouts  1.64 us

profile of v4, /device:TPU:26, one launch (start us, length us, event | category | flops | bytes accessed | tf_op | source)
XLA Modules:
  0.0 48.8 jit_solution(8588325958546195642)
XLA Ops:
  0.0 47.2 %shard_map.46 = f32[8,8,896]{2,1,0:T(8,128)} custom-call(bf16[3,600,256]{2,1,0:T(8,128)(2,1)} %bitcast.6, s32[1,256]{1,0:T(1,128)} %bitcast.9, bf16[3,896]{1,0:T(4,128)(2,1)} %bitcast.7, bf16[3,599]{1,0:T(4,128)(2,1)} %bitcast.8), custom_call_target="tpu_custom_call" | custom-call | tf_op jit(solution)/shard_map/pallas_call | solution.py:265
  47.2 1.6 %copy.6 = f32[8,8,896]{2,1,0:T(8,128)} copy(f32[8,8,896]{2,1,0:T(8,128)} %shard_map.46) | data formatting | bytes 458752

commit v5 on v4

--- a/solution.py
+++ b/solution.py
@@ -58,17 +58,13 @@
     for other in (sib, up, down):
         pl.semaphore_signal(barrier, inc=1, device_id=(t, other), device_id_type=MESH)
     xs[...] = jnp.zeros((8, WIDE), jnp.float32)
-    for cp in locals_:
-        cp.wait()
-
-    maskf = mask_ref[...].astype(jnp.float32)
 
     def templates(comp):
         values = tpl_ref[comp].astype(jnp.float32)
         mean = jnp.sum(values, axis=0, keepdims=True) / LAGS
         centred = values - mean
         energy = jnp.sum(centred * centred, axis=0, keepdims=True)
-        normed = centred * lax.rsqrt(energy + 1e-05) * maskf
+        normed = centred * lax.rsqrt(energy + 1e-05) * mask_ref[...].astype(jnp.float32)
         padded = jnp.concatenate([normed, jnp.zeros((KPAD - LAGS, 256), jnp.float32)], axis=0)
         tf[comp] = padded.T
         for o in range(2):
@@ -85,7 +81,7 @@
         xs[0:3, pl.ds(start, width)] = v
         xs[4:7, pl.ds(start, width)] = v * v
 
-    templates(0)
+    locals_[0].wait()
     pl.semaphore_wait(barrier, 18)
 
     def remote(src, dst, ssem, rsem, dev):
@@ -101,8 +97,10 @@
     ]
     for cp in wcopies:
         begin(cp)
-    templates(1)
-    templates(2)
+    for cp in locals_[1:]:
+        cp.wait()
+    for comp in range(3):
+        templates(comp)
     place(wav_ref[...], pl.multiple_of(t * CHUNK, 128), CHUNK)
     place(tail_ref[...], 8 * CHUNK, LAGS - 1)
     for k in range(1, UNITS):

time: 49 us -> 49 us (level)
  no operation moved by 1% of the time
where the time goes in v5:
time: 49 us; the launch traced here: 48.8 us
  Pallas kernels  47.2 us (96%)
  local copies, waits for them, and re-layouts  1.64 us (3%)
    pallas_call x1, Pallas kernels, per_device(): pl.pallas_call(kernel, out_shape=jax.ShapeDtypeStruct((UNITS, 8, CHUNK),...  47.2 us
    unnamed x1, local copies, waits for them, and re-layouts  1.64 us

profile of v5, /device:TPU:26, one launch (start us, length us, event | category | flops | bytes accessed | tf_op | source)
XLA Modules:
  0.0 48.8 jit_solution(10155853214505129701)
XLA Ops:
  0.0 47.2 %shard_map.46 = f32[8,8,896]{2,1,0:T(8,128)} custom-call(bf16[3,600,256]{2,1,0:T(8,128)(2,1)} %bitcast.6, s32[1,256]{1,0:T(1,128)} %bitcast.9, bf16[3,896]{1,0:T(4,128)(2,1)} %bitcast.7, bf16[3,599]{1,0:T(4,128)(2,1)} %bitcast.8), custom_call_target="tpu_custom_call" | custom-call | tf_op jit(solution)/shard_map/pallas_call | solution.py:263
  47.2 1.6 %copy.6 = f32[8,8,896]{2,1,0:T(8,128)} copy(f32[8,8,896]{2,1,0:T(8,128)} %shard_map.46) | data formatting | bytes 458752
